TPU v7x, 32 devices: a whole 2x2x4 slice. The times are simulated.
32 devices in a mesh: sub: 8 (over z, y), blk: 4 (over x, core).
Axes of the slice: x: 2, y: 2, z: 4, core: 2. Of those that a mesh axis runs over, the one named last changes fastest.
Arguments:
- initial_state: float32 [8, 64, 2048], P('sub', None, 'blk'), may hold values from -6 to 6
- source: bfloat16 [8, 8, 64, 2048], P('sub', None, None, 'blk'), may hold values from -6 to 6
- inverse_diag: float32 [8, 2048], P('sub', 'blk'), may hold values from 0.5 to 0.85
- inverse_off: bfloat16 [8, 2048, 2048], P('sub', None, 'blk'), may hold values from -0.032958984 to 0.032958984
- coupling: float32 [8, 128], P('sub', 'blk'), may hold values from 0.3 to 3
- initial_waves: bfloat16 [8, 128, 512], P('sub', 'blk'), may hold values from -6 to 6
- bucket: int32 [8], P('sub'), may hold values from 0 to 2
- partner: int32 [8, 128], P('sub', 'blk'), may hold values from 0 to 7
- position_of: int32 [8], replicated, may hold values from 0 to 7, each once
Outputs:
- last_state: float32 [8, 64, 2048], P('sub', None, 'blk')
- waveform: float32 [8, 128, 512], P('sub', 'blk')
Inputs may be any that keep to these rules, and one draw needn't show every extreme that they name: A subcircuit of bucket b takes 8 / 2 ** (2 - b) implicit Euler steps. `position_of`: a permutation.
All inputs are finite; a program needn't handle non-finite values.
Results may differ from a plain program's by a relative error of at most 0.0052.
Values may be sent and summed in bfloat16 or wider, within the bound.
A program may use at most 64 MiB of HBM per device.

v0:
```python
import jax
import jax.numpy as jnp
from jax import lax
from jax.sharding import PartitionSpec as P

SWEEPS = 2


def step_count(bucket, refined_points):
    return jnp.where(
        bucket == 0,
        refined_points // 4,
        jnp.where(bucket == 1, refined_points // 2, refined_points),
    ).astype(jnp.int32)


def port_fetch(waves, selector):
    return jnp.einsum(
        "qjr,rjc->qjc",
        selector,
        lax.all_gather(waves, "sub", axis=0, tiled=True),
        preferred_element_type=jnp.float32,
    ).astype(jnp.bfloat16)


def spread_ports(injected, stride):
    padded = jnp.pad(injected[..., None], [(0, 0)] * injected.ndim + [(0, stride - 1)])
    return padded.reshape(injected.shape[:-1] + (injected.shape[-1] * stride,))


def run_together(
    initial_state, source, inverse_diag, inverse_off, coupling, step_total, spacing, incoming
):
    sub_dev, corners, node_block = initial_state.shape
    refined_points = source.shape[1]
    ports_block = coupling.shape[1]
    stride = node_block // ports_block
    spacing_float = spacing.astype(jnp.float32)
    driven = incoming.astype(jnp.float32).reshape(sub_dev, ports_block, refined_points, corners)
    points = jnp.arange(refined_points, dtype=jnp.int32)

    def contract(totals, shard_rows):
        return totals + jnp.einsum(
            "qcn,qnm->qcm", shard_rows, inverse_off, preferred_element_type=jnp.float32
        )

    def advance(time_step_index, carried):
        current, sample_times = carried
        fine_index = (time_step_index + 1) * spacing - 1
        chosen = points[None, :] == fine_index[:, None]
        forcing = jnp.einsum(
            "qf,qfcn->qcn", chosen.astype(jnp.bfloat16), source, preferred_element_type=jnp.float32
        )
        injected = coupling[:, :, None] * jnp.einsum(
            "qf,qjfc->qjc", chosen.astype(jnp.float32), driven, precision=lax.Precision.HIGHEST
        )
        spread = spread_ports(jnp.swapaxes(injected, 1, 2), stride)
        loop_argument = (current + spacing_float[:, None, None] * (forcing + spread)).astype(
            jnp.bfloat16
        )
        loop_argument = lax.optimization_barrier(loop_argument)
        diagonal_term = inverse_diag[:, None, :] * loop_argument.astype(jnp.float32)
        updated = contract(diagonal_term, lax.all_gather(loop_argument, "blk", axis=2, tiled=True))
        active = time_step_index < step_total
        updated = jnp.where(active[:, None, None], updated, current)
        port_values = updated.reshape(sub_dev, corners, ports_block, stride)[:, :, :, 0]
        sample_times = lax.dynamic_update_index_in_dim(
            sample_times, port_values, time_step_index, 1
        )
        return (updated, sample_times)

    sample_times = jnp.zeros((sub_dev, refined_points, corners, ports_block), jnp.float32)
    last_state, sample_times = lax.fori_loop(
        0, refined_points, advance, (initial_state, sample_times)
    )
    kept_values = (points[None, :, None] // spacing[:, None, None] == points[None, None, :]).astype(
        jnp.float32
    )
    waveform = jnp.einsum(
        "qfk,qkcp->qpfc", kept_values, sample_times, precision=lax.Precision.HIGHEST
    )
    return (last_state, waveform.reshape(sub_dev, ports_block, refined_points * corners))


def shards(
    initial_state,
    source,
    inverse_diag,
    inverse_off,
    coupling,
    initial_waves,
    bucket,
    partner,
    position_of,
):
    refined_points = source.shape[1]
    subs_all = position_of.shape[0]
    identities = jnp.arange(subs_all, dtype=jnp.int32)
    located = jnp.sum(
        jnp.where(partner[:, :, None] == identities[None, None, :], position_of[None, None, :], 0),
        axis=2,
    )
    selector = (located[:, :, None] == identities[None, None, :]).astype(jnp.bfloat16)
    step_total = step_count(bucket, refined_points)
    spacing = refined_points // step_total
    waves = initial_waves
    for sweep_index in range(SWEEPS):
        incoming = port_fetch(waves, selector)
        last_state, waveform = run_together(
            initial_state,
            source,
            inverse_diag,
            inverse_off,
            coupling,
            step_total,
            spacing,
            incoming,
        )
        waves = waveform.astype(jnp.bfloat16)
    return (last_state, waveform)


def solution(mesh):
    return jax.shard_map(
        shards,
        mesh=mesh,
        in_specs=(
            P("sub", None, "blk"),
            P("sub", None, None, "blk"),
            P("sub", "blk"),
            P("sub", None, "blk"),
            P("sub", "blk"),
            P("sub", "blk", None),
            P("sub"),
            P("sub", "blk"),
            P(),
        ),
        out_specs=(P("sub", None, "blk"), P("sub", "blk", None)),
        check_vma=False,
    )
```

profile of v0, /device:TPU:0, one launch (start us, length us, event | category | flops | bytes accessed | tf_op | source)
XLA Modules:
  0.0 216.6 jit_solution(17633719554943924317)
XLA Ops:
  3.0 32.8 %all_gather.26 = bf16[8,32,512]{2,1,0:T(8,128)(2,1)S(1)} all-gather(bf16[1,32,512]{2,1,0:T(8,128)(2,1)} %param.20), channel_id=1, replica_groups=mesh['sub'=8,'blk'=4] {'sub'}, dimensions={0}, use_global_device_ids=true | all-gather | bytes 294912 | tf_op jit(solution)/shard_map/all_gather | solution.py:21
  36.2 73.8 %while.36 = (s32[]{:T(128)}, f32[1,64,512]{2,1,0:T(8,128)S(1)}, f32[1,8,64,32]{2,3,1,0:T(8,128)S(1)}, s32[1]{0:T(128)}, f32[1,512]{1,0:T(1,128)}, /*index=5*/f32...) while((s32[]{:T(128)}, f32[1,64,512]{2,1,0:T(8,128)S(1)}, ...), condition=%wide.region_2.3_spmd.clone, body=%wide.region_1.2_spmd.clone.sunk | while | flops 135202832 | bytes 13330811 | solution.py:73
  37.4 1.4 fusion.101
  38.9 5.8 %all_gather.32 = bf16[1,64,2048]{2,1,0:T(8,128)(2,1)S(1)} all-gather(bf16[1,64,512]{2,1,0:T(8,128)(2,1)S(1)} %fusion.102), channel_id=1, replica_groups=mesh['sub'=8,'blk'=4] {'blk'}, dimensions={2}, use_global_device_ids=true | all-gather | bytes 327680 | tf_op jit(solution)/shard_map/while/body/eval_jaxpr/all_gather | solution.py:63
  46.6 1.4 fusion.101
  48.1 5.9 %all_gather.32 = bf16[1,64,2048]{2,1,0:T(8,128)(2,1)S(1)} all-gather(bf16[1,64,512]{2,1,0:T(8,128)(2,1)S(1)} %fusion.102), channel_id=1, replica_groups=mesh['sub'=8,'blk'=4] {'blk'}, dimensions={2}, use_global_device_ids=true | all-gather | bytes 327680 | tf_op jit(solution)/shard_map/while/body/eval_jaxpr/all_gather | solution.py:63
  55.8 1.4 fusion.101
  57.3 5.9 %all_gather.32 = bf16[1,64,2048]{2,1,0:T(8,128)(2,1)S(1)} all-gather(bf16[1,64,512]{2,1,0:T(8,128)(2,1)S(1)} %fusion.102), channel_id=1, replica_groups=mesh['sub'=8,'blk'=4] {'blk'}, dimensions={2}, use_global_device_ids=true | all-gather | bytes 327680 | tf_op jit(solution)/shard_map/while/body/eval_jaxpr/all_gather | solution.py:63
  65.1 1.4 fusion.101
  66.6 5.9 %all_gather.32 = bf16[1,64,2048]{2,1,0:T(8,128)(2,1)S(1)} all-gather(bf16[1,64,512]{2,1,0:T(8,128)(2,1)S(1)} %fusion.102), channel_id=1, replica_groups=mesh['sub'=8,'blk'=4] {'blk'}, dimensions={2}, use_global_device_ids=true | all-gather | bytes 327680 | tf_op jit(solution)/shard_map/while/body/eval_jaxpr/all_gather | solution.py:63
  75.8 5.9 %all_gather.32 = bf16[1,64,2048]{2,1,0:T(8,128)(2,1)S(1)} all-gather(bf16[1,64,512]{2,1,0:T(8,128)(2,1)S(1)} %fusion.102), channel_id=1, replica_groups=mesh['sub'=8,'blk'=4] {'blk'}, dimensions={2}, use_global_device_ids=true | all-gather | bytes 327680 | tf_op jit(solution)/shard_map/while/body/eval_jaxpr/all_gather | solution.py:63
  83.5 1.4 fusion.101
  85.0 5.9 %all_gather.32 = bf16[1,64,2048]{2,1,0:T(8,128)(2,1)S(1)} all-gather(bf16[1,64,512]{2,1,0:T(8,128)(2,1)S(1)} %fusion.102), channel_id=1, replica_groups=mesh['sub'=8,'blk'=4] {'blk'}, dimensions={2}, use_global_device_ids=true | all-gather | bytes 327680 | tf_op jit(solution)/shard_map/while/body/eval_jaxpr/all_gather | solution.py:63
  92.8 1.4 fusion.101
  94.3 5.9 %all_gather.32 = bf16[1,64,2048]{2,1,0:T(8,128)(2,1)S(1)} all-gather(bf16[1,64,512]{2,1,0:T(8,128)(2,1)S(1)} %fusion.102), channel_id=1, replica_groups=mesh['sub'=8,'blk'=4] {'blk'}, dimensions={2}, use_global_device_ids=true | all-gather | bytes 327680 | tf_op jit(solution)/shard_map/while/body/eval_jaxpr/all_gather | solution.py:63
  103.5 5.9 %all_gather.32 = bf16[1,64,2048]{2,1,0:T(8,128)(2,1)S(1)} all-gather(bf16[1,64,512]{2,1,0:T(8,128)(2,1)S(1)} %fusion.102), channel_id=1, replica_groups=mesh['sub'=8,'blk'=4] {'blk'}, dimensions={2}, use_global_device_ids=true | all-gather | bytes 327680 | tf_op jit(solution)/shard_map/while/body/eval_jaxpr/all_gather | solution.py:63
  110.5 30.8 %all_gather.27 = bf16[8,32,512]{2,1,0:T(8,128)(2,1)S(1)} all-gather(bf16[1,32,512]{2,1,0:T(8,128)(2,1)S(1)} %convert_element_type.111), channel_id=1, replica_groups=mesh['sub'=8,'blk'=4] {'sub'}, dimensions={0}, use_global_device_ids=true | all-gather | bytes 294912 | tf_op jit(solution)/shard_map/all_gather | solution.py:21
  141.7 73.8 %while.37 = (s32[]{:T(128)}, f32[1,64,512]{2,1,0:T(8,128)S(1)}, f32[1,8,64,32]{2,3,1,0:T(8,128)S(1)}, s32[1]{0:T(128)}, f32[1,512]{1,0:T(1,128)}, /*index=5*/f32...) while((s32[]{:T(128)}, f32[1,64,512]{2,1,0:T(8,128)S(1)}, ...), condition=%wide.region_4.6_spmd.clone, body=%wide.region_3.5_spmd.clone.sunk | while | flops 135202832 | bytes 13330811 | solution.py:73
  143.0 1.4 fusion.111
  144.5 5.8 %all_gather.33 = bf16[1,64,2048]{2,1,0:T(8,128)(2,1)S(1)} all-gather(bf16[1,64,512]{2,1,0:T(8,128)(2,1)S(1)} %fusion.112), channel_id=1, replica_groups=mesh['sub'=8,'blk'=4] {'blk'}, dimensions={2}, use_global_device_ids=true | all-gather | bytes 327680 | tf_op jit(solution)/shard_map/while/body/eval_jaxpr/all_gather | solution.py:63
  153.6 5.9 %all_gather.33 = bf16[1,64,2048]{2,1,0:T(8,128)(2,1)S(1)} all-gather(bf16[1,64,512]{2,1,0:T(8,128)(2,1)S(1)} %fusion.112), channel_id=1, replica_groups=mesh['sub'=8,'blk'=4] {'blk'}, dimensions={2}, use_global_device_ids=true | all-gather | bytes 327680 | tf_op jit(solution)/shard_map/while/body/eval_jaxpr/all_gather | solution.py:63
  161.4 1.4 fusion.111
  162.9 5.9 %all_gather.33 = bf16[1,64,2048]{2,1,0:T(8,128)(2,1)S(1)} all-gather(bf16[1,64,512]{2,1,0:T(8,128)(2,1)S(1)} %fusion.112), channel_id=1, replica_groups=mesh['sub'=8,'blk'=4] {'blk'}, dimensions={2}, use_global_device_ids=true | all-gather | bytes 327680 | tf_op jit(solution)/shard_map/while/body/eval_jaxpr/all_gather | solution.py:63
  170.6 1.4 fusion.111
  172.1 5.9 %all_gather.33 = bf16[1,64,2048]{2,1,0:T(8,128)(2,1)S(1)} all-gather(bf16[1,64,512]{2,1,0:T(8,128)(2,1)S(1)} %fusion.112), channel_id=1, replica_groups=mesh['sub'=8,'blk'=4] {'blk'}, dimensions={2}, use_global_device_ids=true | all-gather | bytes 327680 | tf_op jit(solution)/shard_map/while/body/eval_jaxpr/all_gather | solution.py:63
  179.8 1.4 fusion.111
  181.3 5.9 %all_gather.33 = bf16[1,64,2048]{2,1,0:T(8,128)(2,1)S(1)} all-gather(bf16[1,64,512]{2,1,0:T(8,128)(2,1)S(1)} %fusion.112), channel_id=1, replica_groups=mesh['sub'=8,'blk'=4] {'blk'}, dimensions={2}, use_global_device_ids=true | all-gather | bytes 327680 | tf_op jit(solution)/shard_map/while/body/eval_jaxpr/all_gather | solution.py:63
  189.1 1.4 fusion.111
  190.6 5.9 %all_gather.33 = bf16[1,64,2048]{2,1,0:T(8,128)(2,1)S(1)} all-gather(bf16[1,64,512]{2,1,0:T(8,128)(2,1)S(1)} %fusion.112), channel_id=1, replica_groups=mesh['sub'=8,'blk'=4] {'blk'}, dimensions={2}, use_global_device_ids=true | all-gather | bytes 327680 | tf_op jit(solution)/shard_map/while/body/eval_jaxpr/all_gather | solution.py:63
  198.3 1.4 fusion.111
  199.8 5.9 %all_gather.33 = bf16[1,64,2048]{2,1,0:T(8,128)(2,1)S(1)} all-gather(bf16[1,64,512]{2,1,0:T(8,128)(2,1)S(1)} %fusion.112), channel_id=1, replica_groups=mesh['sub'=8,'blk'=4] {'blk'}, dimensions={2}, use_global_device_ids=true | all-gather | bytes 327680 | tf_op jit(solution)/shard_map/while/body/eval_jaxpr/all_gather | solution.py:63
  209.0 5.9 %all_gather.33 = bf16[1,64,2048]{2,1,0:T(8,128)(2,1)S(1)} all-gather(bf16[1,64,512]{2,1,0:T(8,128)(2,1)S(1)} %fusion.112), channel_id=1, replica_groups=mesh['sub'=8,'blk'=4] {'blk'}, dimensions={2}, use_global_device_ids=true | all-gather | bytes 327680 | tf_op jit(solution)/shard_map/while/body/eval_jaxpr/all_gather | solution.py:63
  (231 shorter events, 39.2 us)
Async XLA Ops:
  36.2 8.5 %copy-start = (bf16[1,2048,512]{2,1,0:T(8,128)(2,1)S(1)}, bf16[1,2048,512]{2,1,0:T(8,128)(2,1)}, u32[]{:S(2)}) copy-start(bf16[1,2048,512]{2,1,0:T(8,128)(2,1)} %get-tuple-element.845) | copy-start | bytes 6291460 | tf_op jit(solution)/shard_map/while
  36.2 8.5 %copy-start.3 = (f32[1,512]{1,0:T(1,128)S(1)}, f32[1,512]{1,0:T(1,128)}, u32[]{:S(2)}) copy-start(f32[1,512]{1,0:T(1,128)} %get-tuple-element.839) | copy-start | bytes 6148 | tf_op jit(solution)/shard_map/while
  45.4 8.6 %copy-start = (bf16[1,2048,512]{2,1,0:T(8,128)(2,1)S(1)}, bf16[1,2048,512]{2,1,0:T(8,128)(2,1)}, u32[]{:S(2)}) copy-start(bf16[1,2048,512]{2,1,0:T(8,128)(2,1)} %get-tuple-element.845) | copy-start | bytes 6291460 | tf_op jit(solution)/shard_map/while
  45.4 8.6 %copy-start.3 = (f32[1,512]{1,0:T(1,128)S(1)}, f32[1,512]{1,0:T(1,128)}, u32[]{:S(2)}) copy-start(f32[1,512]{1,0:T(1,128)} %get-tuple-element.839) | copy-start | bytes 6148 | tf_op jit(solution)/shard_map/while
  54.6 8.6 %copy-start = (bf16[1,2048,512]{2,1,0:T(8,128)(2,1)S(1)}, bf16[1,2048,512]{2,1,0:T(8,128)(2,1)}, u32[]{:S(2)}) copy-start(bf16[1,2048,512]{2,1,0:T(8,128)(2,1)} %get-tuple-element.845) | copy-start | bytes 6291460 | tf_op jit(solution)/shard_map/while
  54.6 8.5 %copy-start.3 = (f32[1,512]{1,0:T(1,128)S(1)}, f32[1,512]{1,0:T(1,128)}, u32[]{:S(2)}) copy-start(f32[1,512]{1,0:T(1,128)} %get-tuple-element.839) | copy-start | bytes 6148 | tf_op jit(solution)/shard_map/while
  63.9 8.6 %copy-start = (bf16[1,2048,512]{2,1,0:T(8,128)(2,1)S(1)}, bf16[1,2048,512]{2,1,0:T(8,128)(2,1)}, u32[]{:S(2)}) copy-start(bf16[1,2048,512]{2,1,0:T(8,128)(2,1)} %get-tuple-element.845) | copy-start | bytes 6291460 | tf_op jit(solution)/shard_map/while
  63.9 8.6 %copy-start.3 = (f32[1,512]{1,0:T(1,128)S(1)}, f32[1,512]{1,0:T(1,128)}, u32[]{:S(2)}) copy-start(f32[1,512]{1,0:T(1,128)} %get-tuple-element.839) | copy-start | bytes 6148 | tf_op jit(solution)/shard_map/while
  73.1 8.6 %copy-start = (bf16[1,2048,512]{2,1,0:T(8,128)(2,1)S(1)}, bf16[1,2048,512]{2,1,0:T(8,128)(2,1)}, u32[]{:S(2)}) copy-start(bf16[1,2048,512]{2,1,0:T(8,128)(2,1)} %get-tuple-element.845) | copy-start | bytes 6291460 | tf_op jit(solution)/shard_map/while
  73.1 8.6 %copy-start.3 = (f32[1,512]{1,0:T(1,128)S(1)}, f32[1,512]{1,0:T(1,128)}, u32[]{:S(2)}) copy-start(f32[1,512]{1,0:T(1,128)} %get-tuple-element.839) | copy-start | bytes 6148 | tf_op jit(solution)/shard_map/while
  82.3 8.6 %copy-start = (bf16[1,2048,512]{2,1,0:T(8,128)(2,1)S(1)}, bf16[1,2048,512]{2,1,0:T(8,128)(2,1)}, u32[]{:S(2)}) copy-start(bf16[1,2048,512]{2,1,0:T(8,128)(2,1)} %get-tuple-element.845) | copy-start | bytes 6291460 | tf_op jit(solution)/shard_map/while
  82.3 8.5 %copy-start.3 = (f32[1,512]{1,0:T(1,128)S(1)}, f32[1,512]{1,0:T(1,128)}, u32[]{:S(2)}) copy-start(f32[1,512]{1,0:T(1,128)} %get-tuple-element.839) | copy-start | bytes 6148 | tf_op jit(solution)/shard_map/while
  91.6 8.6 %copy-start = (bf16[1,2048,512]{2,1,0:T(8,128)(2,1)S(1)}, bf16[1,2048,512]{2,1,0:T(8,128)(2,1)}, u32[]{:S(2)}) copy-start(bf16[1,2048,512]{2,1,0:T(8,128)(2,1)} %get-tuple-element.845) | copy-start | bytes 6291460 | tf_op jit(solution)/shard_map/while
  91.6 8.5 %copy-start.3 = (f32[1,512]{1,0:T(1,128)S(1)}, f32[1,512]{1,0:T(1,128)}, u32[]{:S(2)}) copy-start(f32[1,512]{1,0:T(1,128)} %get-tuple-element.839) | copy-start | bytes 6148 | tf_op jit(solution)/shard_map/while
  100.8 8.6 %copy-start = (bf16[1,2048,512]{2,1,0:T(8,128)(2,1)S(1)}, bf16[1,2048,512]{2,1,0:T(8,128)(2,1)}, u32[]{:S(2)}) copy-start(bf16[1,2048,512]{2,1,0:T(8,128)(2,1)} %get-tuple-element.845) | copy-start | bytes 6291460 | tf_op jit(solution)/shard_map/while
  100.8 8.5 %copy-start.3 = (f32[1,512]{1,0:T(1,128)S(1)}, f32[1,512]{1,0:T(1,128)}, u32[]{:S(2)}) copy-start(f32[1,512]{1,0:T(1,128)} %get-tuple-element.839) | copy-start | bytes 6148 | tf_op jit(solution)/shard_map/while
  141.8 8.5 %copy-start.1 = (bf16[1,2048,512]{2,1,0:T(8,128)(2,1)S(1)}, bf16[1,2048,512]{2,1,0:T(8,128)(2,1)}, u32[]{:S(2)}) copy-start(bf16[1,2048,512]{2,1,0:T(8,128)(2,1)} %get-tuple-element.887) | copy-start | bytes 6291460 | tf_op jit(solution)/shard_map/while
  141.8 8.5 %copy-start.4 = (f32[1,512]{1,0:T(1,128)S(1)}, f32[1,512]{1,0:T(1,128)}, u32[]{:S(2)}) copy-start(f32[1,512]{1,0:T(1,128)} %get-tuple-element.881) | copy-start | bytes 6148 | tf_op jit(solution)/shard_map/while
  150.9 8.6 %copy-start.1 = (bf16[1,2048,512]{2,1,0:T(8,128)(2,1)S(1)}, bf16[1,2048,512]{2,1,0:T(8,128)(2,1)}, u32[]{:S(2)}) copy-start(bf16[1,2048,512]{2,1,0:T(8,128)(2,1)} %get-tuple-element.887) | copy-start | bytes 6291460 | tf_op jit(solution)/shard_map/while
  150.9 8.6 %copy-start.4 = (f32[1,512]{1,0:T(1,128)S(1)}, f32[1,512]{1,0:T(1,128)}, u32[]{:S(2)}) copy-start(f32[1,512]{1,0:T(1,128)} %get-tuple-element.881) | copy-start | bytes 6148 | tf_op jit(solution)/shard_map/while
  160.1 8.6 %copy-start.1 = (bf16[1,2048,512]{2,1,0:T(8,128)(2,1)S(1)}, bf16[1,2048,512]{2,1,0:T(8,128)(2,1)}, u32[]{:S(2)}) copy-start(bf16[1,2048,512]{2,1,0:T(8,128)(2,1)} %get-tuple-element.887) | copy-start | bytes 6291460 | tf_op jit(solution)/shard_map/while
  160.2 8.6 %copy-start.4 = (f32[1,512]{1,0:T(1,128)S(1)}, f32[1,512]{1,0:T(1,128)}, u32[]{:S(2)}) copy-start(f32[1,512]{1,0:T(1,128)} %get-tuple-element.881) | copy-start | bytes 6148 | tf_op jit(solution)/shard_map/while
  169.4 8.6 %copy-start.1 = (bf16[1,2048,512]{2,1,0:T(8,128)(2,1)S(1)}, bf16[1,2048,512]{2,1,0:T(8,128)(2,1)}, u32[]{:S(2)}) copy-start(bf16[1,2048,512]{2,1,0:T(8,128)(2,1)} %get-tuple-element.887) | copy-start | bytes 6291460 | tf_op jit(solution)/shard_map/while
  169.4 8.6 %copy-start.4 = (f32[1,512]{1,0:T(1,128)S(1)}, f32[1,512]{1,0:T(1,128)}, u32[]{:S(2)}) copy-start(f32[1,512]{1,0:T(1,128)} %get-tuple-element.881) | copy-start | bytes 6148 | tf_op jit(solution)/shard_map/while
  178.6 8.6 %copy-start.1 = (bf16[1,2048,512]{2,1,0:T(8,128)(2,1)S(1)}, bf16[1,2048,512]{2,1,0:T(8,128)(2,1)}, u32[]{:S(2)}) copy-start(bf16[1,2048,512]{2,1,0:T(8,128)(2,1)} %get-tuple-element.887) | copy-start | bytes 6291460 | tf_op jit(solution)/shard_map/while
  178.6 8.6 %copy-start.4 = (f32[1,512]{1,0:T(1,128)S(1)}, f32[1,512]{1,0:T(1,128)}, u32[]{:S(2)}) copy-start(f32[1,512]{1,0:T(1,128)} %get-tuple-element.881) | copy-start | bytes 6148 | tf_op jit(solution)/shard_map/while
  187.9 8.6 %copy-start.1 = (bf16[1,2048,512]{2,1,0:T(8,128)(2,1)S(1)}, bf16[1,2048,512]{2,1,0:T(8,128)(2,1)}, u32[]{:S(2)}) copy-start(bf16[1,2048,512]{2,1,0:T(8,128)(2,1)} %get-tuple-element.887) | copy-start | bytes 6291460 | tf_op jit(solution)/shard_map/while
  187.9 8.6 %copy-start.4 = (f32[1,512]{1,0:T(1,128)S(1)}, f32[1,512]{1,0:T(1,128)}, u32[]{:S(2)}) copy-start(f32[1,512]{1,0:T(1,128)} %get-tuple-element.881) | copy-start | bytes 6148 | tf_op jit(solution)/shard_map/while
  197.1 8.6 %copy-start.1 = (bf16[1,2048,512]{2,1,0:T(8,128)(2,1)S(1)}, bf16[1,2048,512]{2,1,0:T(8,128)(2,1)}, u32[]{:S(2)}) copy-start(bf16[1,2048,512]{2,1,0:T(8,128)(2,1)} %get-tuple-element.887) | copy-start | bytes 6291460 | tf_op jit(solution)/shard_map/while
  197.1 8.6 %copy-start.4 = (f32[1,512]{1,0:T(1,128)S(1)}, f32[1,512]{1,0:T(1,128)}, u32[]{:S(2)}) copy-start(f32[1,512]{1,0:T(1,128)} %get-tuple-element.881) | copy-start | bytes 6148 | tf_op jit(solution)/shard_map/while
  206.3 8.6 %copy-start.1 = (bf16[1,2048,512]{2,1,0:T(8,128)(2,1)S(1)}, bf16[1,2048,512]{2,1,0:T(8,128)(2,1)}, u32[]{:S(2)}) copy-start(bf16[1,2048,512]{2,1,0:T(8,128)(2,1)} %get-tuple-element.887) | copy-start | bytes 6291460 | tf_op jit(solution)/shard_map/while
  206.3 8.6 %copy-start.4 = (f32[1,512]{1,0:T(1,128)S(1)}, f32[1,512]{1,0:T(1,128)}, u32[]{:S(2)}) copy-start(f32[1,512]{1,0:T(1,128)} %get-tuple-element.881) | copy-start | bytes 6148 | tf_op jit(solution)/shard_map/while
  (1 other events, 1.0 us)
where the time goes:
time: 217 us
  blocking collectives  157 us (72%)
  matrix products  35 us (16%)
  other arithmetic  15 us (7%)
  local copies, waits for them, and re-layouts  6.51 us (3%)
    all_gather x16, blocking collectives, advance(): lax.all_gather(loop_argument, 'blk', axis=2, tiled=True)  93.5 us
    all_gather x2, blocking collectives, port_fetch(): lax.all_gather(waves, 'sub', axis=0, tiled=True)  63.5 us
    dot_general x16, matrix products, advance(): jnp.einsum('qf,qfcn->qcn', chosen.astype(jnp.bfloat16), source, preferred...  23.2 us
    mul x16, other arithmetic, advance(): coupling[:, :, None]  13.5 us
    dot_general x16, matrix products, contract(): jnp.einsum('qcn,qnm->qcm', shard_rows, inverse_off, preferred_element_typ...  7.7 us

commit v1 on v0

--- a/solution.py
+++ b/solution.py
@@ -4,6 +4,22 @@
 from jax.sharding import PartitionSpec as P
 
 SWEEPS = 2
+
+
+def product_in_turn(x, axis, dim, term):
+    length, position, rows = (lax.axis_size(axis), lax.axis_index(axis), x.shape[dim])
+    right = [(i, (i + 1) % length) for i in range(length)]
+    left = [(i, (i - 1) % length) for i in range(length)]
+    half = length // 2
+    from_left = from_right = x
+    total = term(x, position * rows)
+    for step in range(1, half + 1):
+        from_left = lax.ppermute(from_left, axis, right)
+        if step < length - half:
+            from_right = lax.ppermute(from_right, axis, left)
+            total = total + term(from_right, (position + step) % length * rows)
+        total = total + term(from_left, (position - step) % length * rows)
+    return total
 
 
 def step_count(bucket, refined_points):
@@ -15,11 +31,16 @@
 
 
 def port_fetch(waves, selector):
-    return jnp.einsum(
-        "qjr,rjc->qjc",
-        selector,
-        lax.all_gather(waves, "sub", axis=0, tiled=True),
-        preferred_element_type=jnp.float32,
+    return product_in_turn(
+        waves,
+        "sub",
+        0,
+        lambda shard, start: jnp.einsum(
+            "qjr,rjc->qjc",
+            lax.dynamic_slice_in_dim(selector, start, shard.shape[0], axis=2),
+            shard,
+            preferred_element_type=jnp.float32,
+        ),
     ).astype(jnp.bfloat16)
 
 

time: 217 us -> 207 us (0.954)
  blocking collectives: 157 us -> 93.6 us
  starting transfers between devices: 0 us -> 29.7 us
  waiting for transfers between devices: 0 us -> 22.9 us
    all_gather x2 -> x0, blocking collectives: 63.5 us -> none  [port_fetch(): lax.all_gather(waves, 'sub', axis=0, tiled=True)]
    ppermute x0 -> x14, starting transfers between devices: none -> 29.7 us  [the longest x6 26.6 us: product_in_turn(): from_right = lax.ppermute(from_right, axis, left)]
    ppermute x0 -> x14, waiting for transfers between devices: none -> 22.9 us  [the longest x8 22.6 us: product_in_turn(): from_left = lax.ppermute(from_left, axis, right)]
  transfers between devices with their start and end apart: 0 -> 14, of which waited for: 0 -> 9; matrix products, arithmetic and copies ran while one was open for 0% -> 0% of each run, Pallas kernels for 0% -> 0%
where the time goes in v1:
time: 207 us; the launch traced here: 206 us
  blocking collectives  93.6 us (45%)
  matrix products  34.5 us (17%)
  starting transfers between devices  29.7 us (14%)
  waiting for transfers between devices  22.9 us (11%)
  other arithmetic  15.9 us (8%)
  local copies, waits for them, and re-layouts  6.61 us (3%)
    all_gather x16, blocking collectives, advance(): lax.all_gather(loop_argument, 'blk', axis=2, tiled=True)  93.6 us
    ppermute x6, starting transfers between devices, product_in_turn(): from_right = lax.ppermute(from_right, axis, left)  26.6 us
    dot_general x16, matrix products, advance(): jnp.einsum('qf,qfcn->qcn', chosen.astype(jnp.bfloat16), source, preferred...  23.2 us
    ppermute x8, waiting for transfers between devices, product_in_turn(): from_left = lax.ppermute(from_left, axis, right)  22.6 us
    mul x16, other arithmetic, advance(): coupling[:, :, None]  13.5 us
    dot_general x16, matrix products, contract(): jnp.einsum('qcn,qnm->qcm', shard_rows, inverse_off, preferred_element_typ...  7.7 us
  transfers between devices with their start and end apart: 14, of which 9 were waited for; matrix products, arithmetic and copies ran while one was open for 0% of the time, Pallas kernels for 0%

profile of v1, /device:TPU:0, one launch (start us, length us, event | category | flops | bytes accessed | tf_op | source)
XLA Modules:
  0.0 206.4 jit_solution(12971529277287693106)
XLA Ops:
  1.5 3.0 %collective-permute-start.1 = (bf16[1,32,512]{2,1,0:T(8,128)(2,1)}, bf16[1,32,512]{2,1,0:T(8,128)(2,1)S(1)}, u32[]{:S(2)}, u32[]{:S(2)}) collective-permute-start(bf16[1,32,512]{2,1,0:T(8,128)(2,1)} %param.20), channel_id=1, source_target_pairs={{0,4},{4,8},{8,12},{12,16},{16,20},{20,24},{24,28},{28,0},{1,5},{5... | collective-permute-start | bytes 98312 | tf_op jit(solution)/shard_map/ppermute | solution.py:17
  4.5 3.0 %collective-permute-start = (bf16[1,32,512]{2,1,0:T(8,128)(2,1)}, bf16[1,32,512]{2,1,0:T(8,128)(2,1)S(1)}, u32[]{:S(2)}, u32[]{:S(2)}) collective-permute-start(bf16[1,32,512]{2,1,0:T(8,128)(2,1)} %param.20), channel_id=1, source_target_pairs={{0,28},{4,0},{8,4},{12,8},{16,12},{20,16},{24,20},{28,24},{1,29},{... | collective-permute-start | bytes 98312 | tf_op jit(solution)/shard_map/ppermute | solution.py:19
  9.8 4.6 %collective-permute-start.2 = (bf16[1,32,512]{2,1,0:T(8,128)(2,1)S(1)}, bf16[1,32,512]{2,1,0:T(8,128)(2,1)S(1)}, u32[]{:S(2)}, u32[]{:S(2)}) collective-permute-start(bf16[1,32,512]{2,1,0:T(8,128)(2,1)S(1)} %collective-permute-done), channel_id=1, source_target_pairs={{0,28},{4,0},{8,4},{12,8},{16,12},{20,16},{24,20},{28,24},{1,29},{... | collective-permute-start | bytes 98312 | tf_op jit(solution)/shard_map/ppermute | solution.py:19
  14.5 1.8 collective-permute-done.3
  17.0 4.8 %collective-permute-start.4 = (bf16[1,32,512]{2,1,0:T(8,128)(2,1)S(1)}, bf16[1,32,512]{2,1,0:T(8,128)(2,1)S(1)}, u32[]{:S(2)}, u32[]{:S(2)}) collective-permute-start(bf16[1,32,512]{2,1,0:T(8,128)(2,1)S(1)} %collective-permute-done.2), channel_id=1, source_target_pairs={{0,28},{4,0},{8,4},{12,8},{16,12},{20,16},{24,20},{28,24},{1,29},{... | collective-permute-start | bytes 98312 | tf_op jit(solution)/shard_map/ppermute | solution.py:19
  23.4 6.1 %collective-permute-done.6 = bf16[1,32,512]{2,1,0:T(8,128)(2,1)S(1)} collective-permute-done((bf16[1,32,512]{2,1,0:T(8,128)(2,1)S(1)}, bf16[1,32,512]{2,1,0:T(8,128)(2,1)S(1)}, u32[]{:S(2)}, u32[]{:S(2)}) %collective-permute-start.6) | collective-permute-done | bytes 32800 | tf_op jit(solution)/shard_map/ppermute | solution.py:17
  30.5 73.9 %while.36 = (s32[]{:T(128)}, f32[1,64,512]{2,1,0:T(8,128)S(1)}, f32[1,8,64,32]{2,3,1,0:T(8,128)S(1)}, s32[1]{0:T(128)}, f32[1,512]{1,0:T(1,128)}, /*index=5*/f32...) while((s32[]{:T(128)}, f32[1,64,512]{2,1,0:T(8,128)S(1)}, ...), condition=%wide.region_2.3_spmd.clone, body=%wide.region_1.2_spmd.clone.sunk | while | flops 135202832 | bytes 13330811 | solution.py:94
  31.7 1.4 fusion.126
  33.2 5.9 %all_gather.24 = bf16[1,64,2048]{2,1,0:T(8,128)(2,1)S(1)} all-gather(bf16[1,64,512]{2,1,0:T(8,128)(2,1)S(1)} %fusion.127), channel_id=1, replica_groups=mesh['sub'=8,'blk'=4] {'blk'}, dimensions={2}, use_global_device_ids=true | all-gather | bytes 327680 | tf_op jit(solution)/shard_map/while/body/eval_jaxpr/all_gather | solution.py:84
  42.5 5.9 %all_gather.24 = bf16[1,64,2048]{2,1,0:T(8,128)(2,1)S(1)} all-gather(bf16[1,64,512]{2,1,0:T(8,128)(2,1)S(1)} %fusion.127), channel_id=1, replica_groups=mesh['sub'=8,'blk'=4] {'blk'}, dimensions={2}, use_global_device_ids=true | all-gather | bytes 327680 | tf_op jit(solution)/shard_map/while/body/eval_jaxpr/all_gather | solution.py:84
  51.7 5.9 %all_gather.24 = bf16[1,64,2048]{2,1,0:T(8,128)(2,1)S(1)} all-gather(bf16[1,64,512]{2,1,0:T(8,128)(2,1)S(1)} %fusion.127), channel_id=1, replica_groups=mesh['sub'=8,'blk'=4] {'blk'}, dimensions={2}, use_global_device_ids=true | all-gather | bytes 327680 | tf_op jit(solution)/shard_map/while/body/eval_jaxpr/all_gather | solution.py:84
  61.0 5.9 %all_gather.24 = bf16[1,64,2048]{2,1,0:T(8,128)(2,1)S(1)} all-gather(bf16[1,64,512]{2,1,0:T(8,128)(2,1)S(1)} %fusion.127), channel_id=1, replica_groups=mesh['sub'=8,'blk'=4] {'blk'}, dimensions={2}, use_global_device_ids=true | all-gather | bytes 327680 | tf_op jit(solution)/shard_map/while/body/eval_jaxpr/all_gather | solution.py:84
  70.2 5.9 %all_gather.24 = bf16[1,64,2048]{2,1,0:T(8,128)(2,1)S(1)} all-gather(bf16[1,64,512]{2,1,0:T(8,128)(2,1)S(1)} %fusion.127), channel_id=1, replica_groups=mesh['sub'=8,'blk'=4] {'blk'}, dimensions={2}, use_global_device_ids=true | all-gather | bytes 327680 | tf_op jit(solution)/shard_map/while/body/eval_jaxpr/all_gather | solution.py:84
  79.4 5.9 %all_gather.24 = bf16[1,64,2048]{2,1,0:T(8,128)(2,1)S(1)} all-gather(bf16[1,64,512]{2,1,0:T(8,128)(2,1)S(1)} %fusion.127), channel_id=1, replica_groups=mesh['sub'=8,'blk'=4] {'blk'}, dimensions={2}, use_global_device_ids=true | all-gather | bytes 327680 | tf_op jit(solution)/shard_map/while/body/eval_jaxpr/all_gather | solution.py:84
  88.7 5.9 %all_gather.24 = bf16[1,64,2048]{2,1,0:T(8,128)(2,1)S(1)} all-gather(bf16[1,64,512]{2,1,0:T(8,128)(2,1)S(1)} %fusion.127), channel_id=1, replica_groups=mesh['sub'=8,'blk'=4] {'blk'}, dimensions={2}, use_global_device_ids=true | all-gather | bytes 327680 | tf_op jit(solution)/shard_map/while/body/eval_jaxpr/all_gather | solution.py:84
  97.9 5.9 %all_gather.24 = bf16[1,64,2048]{2,1,0:T(8,128)(2,1)S(1)} all-gather(bf16[1,64,512]{2,1,0:T(8,128)(2,1)S(1)} %fusion.127), channel_id=1, replica_groups=mesh['sub'=8,'blk'=4] {'blk'}, dimensions={2}, use_global_device_ids=true | all-gather | bytes 327680 | tf_op jit(solution)/shard_map/while/body/eval_jaxpr/all_gather | solution.py:84
  104.9 4.7 %collective-permute-start.7 = (bf16[1,32,512]{2,1,0:T(8,128)(2,1)S(1)}, bf16[1,32,512]{2,1,0:T(8,128)(2,1)S(1)}, u32[]{:S(2)}, u32[]{:S(2)}) collective-permute-start(bf16[1,32,512]{2,1,0:T(8,128)(2,1)S(1)} %convert_element_type.109), channel_id=1, source_target_pairs={{0,28},{4,0},{8,4},{12,8},{16,12},{20,16},{24,20},{28,24},{1,29},{... | collective-permute-start | bytes 98312 | tf_op jit(solution)/shard_map/ppermute | solution.py:19
  109.6 1.9 collective-permute-done.8
  111.5 4.7 %collective-permute-start.9 = (bf16[1,32,512]{2,1,0:T(8,128)(2,1)S(1)}, bf16[1,32,512]{2,1,0:T(8,128)(2,1)S(1)}, u32[]{:S(2)}, u32[]{:S(2)}) collective-permute-start(bf16[1,32,512]{2,1,0:T(8,128)(2,1)S(1)} %collective-permute-done.7), channel_id=1, source_target_pairs={{0,28},{4,0},{8,4},{12,8},{16,12},{20,16},{24,20},{28,24},{1,29},{... | collective-permute-start | bytes 98312 | tf_op jit(solution)/shard_map/ppermute | solution.py:19
  116.2 1.9 collective-permute-done.10
  118.1 4.7 %collective-permute-start.11 = (bf16[1,32,512]{2,1,0:T(8,128)(2,1)S(1)}, bf16[1,32,512]{2,1,0:T(8,128)(2,1)S(1)}, u32[]{:S(2)}, u32[]{:S(2)}) collective-permute-start(bf16[1,32,512]{2,1,0:T(8,128)(2,1)S(1)} %collective-permute-done.9), channel_id=1, source_target_pairs={{0,28},{4,0},{8,4},{12,8},{16,12},{20,16},{24,20},{28,24},{1,29},{... | collective-permute-start | bytes 98312 | tf_op jit(solution)/shard_map/ppermute | solution.py:19
  122.8 1.9 collective-permute-done.12
  124.8 6.5 %collective-permute-done.13 = bf16[1,32,512]{2,1,0:T(8,128)(2,1)S(1)} collective-permute-done((bf16[1,32,512]{2,1,0:T(8,128)(2,1)S(1)}, bf16[1,32,512]{2,1,0:T(8,128)(2,1)S(1)}, u32[]{:S(2)}, u32[]{:S(2)}) %collective-permute-start.13) | collective-permute-done | bytes 32800 | tf_op jit(solution)/shard_map/ppermute | solution.py:17
  131.6 73.8 %while.37 = (s32[]{:T(128)}, f32[1,64,512]{2,1,0:T(8,128)S(1)}, f32[1,8,64,32]{2,3,1,0:T(8,128)S(1)}, s32[1]{0:T(128)}, f32[1,512]{1,0:T(1,128)}, /*index=5*/f32...) while((s32[]{:T(128)}, f32[1,64,512]{2,1,0:T(8,128)S(1)}, ...), condition=%wide.region_4.6_spmd.clone, body=%wide.region_3.5_spmd.clone.sunk | while | flops 135202832 | bytes 13330811 | solution.py:94
  134.3 5.8 %all_gather.25 = bf16[1,64,2048]{2,1,0:T(8,128)(2,1)S(1)} all-gather(bf16[1,64,512]{2,1,0:T(8,128)(2,1)S(1)} %fusion.137), channel_id=1, replica_groups=mesh['sub'=8,'blk'=4] {'blk'}, dimensions={2}, use_global_device_ids=true | all-gather | bytes 327680 | tf_op jit(solution)/shard_map/while/body/eval_jaxpr/all_gather | solution.py:84
  143.4 5.9 %all_gather.25 = bf16[1,64,2048]{2,1,0:T(8,128)(2,1)S(1)} all-gather(bf16[1,64,512]{2,1,0:T(8,128)(2,1)S(1)} %fusion.137), channel_id=1, replica_groups=mesh['sub'=8,'blk'=4] {'blk'}, dimensions={2}, use_global_device_ids=true | all-gather | bytes 327680 | tf_op jit(solution)/shard_map/while/body/eval_jaxpr/all_gather | solution.py:84
  152.7 5.9 %all_gather.25 = bf16[1,64,2048]{2,1,0:T(8,128)(2,1)S(1)} all-gather(bf16[1,64,512]{2,1,0:T(8,128)(2,1)S(1)} %fusion.137), channel_id=1, replica_groups=mesh['sub'=8,'blk'=4] {'blk'}, dimensions={2}, use_global_device_ids=true | all-gather | bytes 327680 | tf_op jit(solution)/shard_map/while/body/eval_jaxpr/all_gather | solution.py:84
  161.9 5.9 %all_gather.25 = bf16[1,64,2048]{2,1,0:T(8,128)(2,1)S(1)} all-gather(bf16[1,64,512]{2,1,0:T(8,128)(2,1)S(1)} %fusion.137), channel_id=1, replica_groups=mesh['sub'=8,'blk'=4] {'blk'}, dimensions={2}, use_global_device_ids=true | all-gather | bytes 327680 | tf_op jit(solution)/shard_map/while/body/eval_jaxpr/all_gather | solution.py:84
  171.2 5.9 %all_gather.25 = bf16[1,64,2048]{2,1,0:T(8,128)(2,1)S(1)} all-gather(bf16[1,64,512]{2,1,0:T(8,128)(2,1)S(1)} %fusion.137), channel_id=1, replica_groups=mesh['sub'=8,'blk'=4] {'blk'}, dimensions={2}, use_global_device_ids=true | all-gather | bytes 327680 | tf_op jit(solution)/shard_map/while/body/eval_jaxpr/all_gather | solution.py:84
  180.4 5.9 %all_gather.25 = bf16[1,64,2048]{2,1,0:T(8,128)(2,1)S(1)} all-gather(bf16[1,64,512]{2,1,0:T(8,128)(2,1)S(1)} %fusion.137), channel_id=1, replica_groups=mesh['sub'=8,'blk'=4] {'blk'}, dimensions={2}, use_global_device_ids=true | all-gather | bytes 327680 | tf_op jit(solution)/shard_map/while/body/eval_jaxpr/all_gather | solution.py:84
  189.6 5.9 %all_gather.25 = bf16[1,64,2048]{2,1,0:T(8,128)(2,1)S(1)} all-gather(bf16[1,64,512]{2,1,0:T(8,128)(2,1)S(1)} %fusion.137), channel_id=1, replica_groups=mesh['sub'=8,'blk'=4] {'blk'}, dimensions={2}, use_global_device_ids=true | all-gather | bytes 327680 | tf_op jit(solution)/shard_map/while/body/eval_jaxpr/all_gather | solution.py:84
  198.9 5.9 %all_gather.25 = bf16[1,64,2048]{2,1,0:T(8,128)(2,1)S(1)} all-gather(bf16[1,64,512]{2,1,0:T(8,128)(2,1)S(1)} %fusion.137), channel_id=1, replica_groups=mesh['sub'=8,'blk'=4] {'blk'}, dimensions={2}, use_global_device_ids=true | all-gather | bytes 327680 | tf_op jit(solution)/shard_map/while/body/eval_jaxpr/all_gather | solution.py:84
  (257 shorter events, 58.4 us)
Async XLA Ops:
  1.5 8.1 %collective-permute-start.1 = (bf16[1,32,512]{2,1,0:T(8,128)(2,1)}, bf16[1,32,512]{2,1,0:T(8,128)(2,1)S(1)}, u32[]{:S(2)}, u32[]{:S(2)}) collective-permute-start(bf16[1,32,512]{2,1,0:T(8,128)(2,1)} %param.20), channel_id=1, source_target_pairs={{0,4},{4,8},{8,12},{12,16},{16,20},{20,24},{24,28},{28,0},{1,5},{5... | collective-permute-start | bytes 98312 | tf_op jit(solution)/shard_map/ppermute | solution.py:17
  4.5 5.3 %collective-permute-start = (bf16[1,32,512]{2,1,0:T(8,128)(2,1)}, bf16[1,32,512]{2,1,0:T(8,128)(2,1)S(1)}, u32[]{:S(2)}, u32[]{:S(2)}) collective-permute-start(bf16[1,32,512]{2,1,0:T(8,128)(2,1)} %param.20), channel_id=1, source_target_pairs={{0,28},{4,0},{8,4},{12,8},{16,12},{20,16},{24,20},{28,24},{1,29},{... | collective-permute-start | bytes 98312 | tf_op jit(solution)/shard_map/ppermute | solution.py:19
  9.7 6.6 %collective-permute-start.3 = (bf16[1,32,512]{2,1,0:T(8,128)(2,1)S(1)}, bf16[1,32,512]{2,1,0:T(8,128)(2,1)S(1)}, u32[]{:S(2)}, u32[]{:S(2)}) collective-permute-start(bf16[1,32,512]{2,1,0:T(8,128)(2,1)S(1)} %collective-permute-done.1), channel_id=1, source_target_pairs={{0,4},{4,8},{8,12},{12,16},{16,20},{20,24},{24,28},{28,0},{1,5},{5... | collective-permute-start | bytes 98312 | tf_op jit(solution)/shard_map/ppermute | solution.py:17
  9.8 7.2 %collective-permute-start.2 = (bf16[1,32,512]{2,1,0:T(8,128)(2,1)S(1)}, bf16[1,32,512]{2,1,0:T(8,128)(2,1)S(1)}, u32[]{:S(2)}, u32[]{:S(2)}) collective-permute-start(bf16[1,32,512]{2,1,0:T(8,128)(2,1)S(1)} %collective-permute-done), channel_id=1, source_target_pairs={{0,28},{4,0},{8,4},{12,8},{16,12},{20,16},{24,20},{28,24},{1,29},{... | collective-permute-start | bytes 98312 | tf_op jit(solution)/shard_map/ppermute | solution.py:19
  16.3 6.6 %collective-permute-start.5 = (bf16[1,32,512]{2,1,0:T(8,128)(2,1)S(1)}, bf16[1,32,512]{2,1,0:T(8,128)(2,1)S(1)}, u32[]{:S(2)}, u32[]{:S(2)}) collective-permute-start(bf16[1,32,512]{2,1,0:T(8,128)(2,1)S(1)} %collective-permute-done.3), channel_id=1, source_target_pairs={{0,4},{4,8},{8,12},{12,16},{16,20},{20,24},{24,28},{28,0},{1,5},{5... | collective-permute-start | bytes 98312 | tf_op jit(solution)/shard_map/ppermute | solution.py:17
  17.0 6.4 %collective-permute-start.4 = (bf16[1,32,512]{2,1,0:T(8,128)(2,1)S(1)}, bf16[1,32,512]{2,1,0:T(8,128)(2,1)S(1)}, u32[]{:S(2)}, u32[]{:S(2)}) collective-permute-start(bf16[1,32,512]{2,1,0:T(8,128)(2,1)S(1)} %collective-permute-done.2), channel_id=1, source_target_pairs={{0,28},{4,0},{8,4},{12,8},{16,12},{20,16},{24,20},{28,24},{1,29},{... | collective-permute-start | bytes 98312 | tf_op jit(solution)/shard_map/ppermute | solution.py:19
  22.9 6.6 %collective-permute-start.6 = (bf16[1,32,512]{2,1,0:T(8,128)(2,1)S(1)}, bf16[1,32,512]{2,1,0:T(8,128)(2,1)S(1)}, u32[]{:S(2)}, u32[]{:S(2)}) collective-permute-start(bf16[1,32,512]{2,1,0:T(8,128)(2,1)S(1)} %collective-permute-done.5), channel_id=1, source_target_pairs={{0,4},{4,8},{8,12},{12,16},{16,20},{20,24},{24,28},{28,0},{1,5},{5... | collective-permute-start | bytes 98312 | tf_op jit(solution)/shard_map/ppermute | solution.py:17
  30.5 8.6 %copy-start = (bf16[1,2048,512]{2,1,0:T(8,128)(2,1)S(1)}, bf16[1,2048,512]{2,1,0:T(8,128)(2,1)}, u32[]{:S(2)}) copy-start(bf16[1,2048,512]{2,1,0:T(8,128)(2,1)} %get-tuple-element.853) | copy-start | bytes 6291460 | tf_op jit(solution)/shard_map/while
  30.5 8.6 %copy-start.3 = (f32[1,512]{1,0:T(1,128)S(1)}, f32[1,512]{1,0:T(1,128)}, u32[]{:S(2)}) copy-start(f32[1,512]{1,0:T(1,128)} %get-tuple-element.847) | copy-start | bytes 6148 | tf_op jit(solution)/shard_map/while
  39.8 8.6 %copy-start = (bf16[1,2048,512]{2,1,0:T(8,128)(2,1)S(1)}, bf16[1,2048,512]{2,1,0:T(8,128)(2,1)}, u32[]{:S(2)}) copy-start(bf16[1,2048,512]{2,1,0:T(8,128)(2,1)} %get-tuple-element.853) | copy-start | bytes 6291460 | tf_op jit(solution)/shard_map/while
  49.0 8.6 %copy-start = (bf16[1,2048,512]{2,1,0:T(8,128)(2,1)S(1)}, bf16[1,2048,512]{2,1,0:T(8,128)(2,1)}, u32[]{:S(2)}) copy-start(bf16[1,2048,512]{2,1,0:T(8,128)(2,1)} %get-tuple-element.853) | copy-start | bytes 6291460 | tf_op jit(solution)/shard_map/while
  58.3 8.6 %copy-start = (bf16[1,2048,512]{2,1,0:T(8,128)(2,1)S(1)}, bf16[1,2048,512]{2,1,0:T(8,128)(2,1)}, u32[]{:S(2)}) copy-start(bf16[1,2048,512]{2,1,0:T(8,128)(2,1)} %get-tuple-element.853) | copy-start | bytes 6291460 | tf_op jit(solution)/shard_map/while
  67.5 8.6 %copy-start = (bf16[1,2048,512]{2,1,0:T(8,128)(2,1)S(1)}, bf16[1,2048,512]{2,1,0:T(8,128)(2,1)}, u32[]{:S(2)}) copy-start(bf16[1,2048,512]{2,1,0:T(8,128)(2,1)} %get-tuple-element.853) | copy-start | bytes 6291460 | tf_op jit(solution)/shard_map/while
  76.7 8.6 %copy-start = (bf16[1,2048,512]{2,1,0:T(8,128)(2,1)S(1)}, bf16[1,2048,512]{2,1,0:T(8,128)(2,1)}, u32[]{:S(2)}) copy-start(bf16[1,2048,512]{2,1,0:T(8,128)(2,1)} %get-tuple-element.853) | copy-start | bytes 6291460 | tf_op jit(solution)/shard_map/while
  86.0 8.6 %copy-start = (bf16[1,2048,512]{2,1,0:T(8,128)(2,1)S(1)}, bf16[1,2048,512]{2,1,0:T(8,128)(2,1)}, u32[]{:S(2)}) copy-start(bf16[1,2048,512]{2,1,0:T(8,128)(2,1)} %get-tuple-element.853) | copy-start | bytes 6291460 | tf_op jit(solution)/shard_map/while
  95.2 8.6 %copy-start = (bf16[1,2048,512]{2,1,0:T(8,128)(2,1)S(1)}, bf16[1,2048,512]{2,1,0:T(8,128)(2,1)}, u32[]{:S(2)}) copy-start(bf16[1,2048,512]{2,1,0:T(8,128)(2,1)} %get-tuple-element.853) | copy-start | bytes 6291460 | tf_op jit(solution)/shard_map/while
  104.8 6.7 %collective-permute-start.8 = (bf16[1,32,512]{2,1,0:T(8,128)(2,1)S(1)}, bf16[1,32,512]{2,1,0:T(8,128)(2,1)S(1)}, u32[]{:S(2)}, u32[]{:S(2)}) collective-permute-start(bf16[1,32,512]{2,1,0:T(8,128)(2,1)S(1)} %convert_element_type.109), channel_id=1, source_target_pairs={{0,4},{4,8},{8,12},{12,16},{16,20},{20,24},{24,28},{28,0},{1,5},{5... | collective-permute-start | bytes 98312 | tf_op jit(solution)/shard_map/ppermute | solution.py:17
  104.9 6.6 %collective-permute-start.7 = (bf16[1,32,512]{2,1,0:T(8,128)(2,1)S(1)}, bf16[1,32,512]{2,1,0:T(8,128)(2,1)S(1)}, u32[]{:S(2)}, u32[]{:S(2)}) collective-permute-start(bf16[1,32,512]{2,1,0:T(8,128)(2,1)S(1)} %convert_element_type.109), channel_id=1, source_target_pairs={{0,28},{4,0},{8,4},{12,8},{16,12},{20,16},{24,20},{28,24},{1,29},{... | collective-permute-start | bytes 98312 | tf_op jit(solution)/shard_map/ppermute | solution.py:19
  111.5 6.6 %collective-permute-start.10 = (bf16[1,32,512]{2,1,0:T(8,128)(2,1)S(1)}, bf16[1,32,512]{2,1,0:T(8,128)(2,1)S(1)}, u32[]{:S(2)}, u32[]{:S(2)}) collective-permute-start(bf16[1,32,512]{2,1,0:T(8,128)(2,1)S(1)} %collective-permute-done.8), channel_id=1, source_target_pairs={{0,4},{4,8},{8,12},{12,16},{16,20},{20,24},{24,28},{28,0},{1,5},{5... | collective-permute-start | bytes 98312 | tf_op jit(solution)/shard_map/ppermute | solution.py:17
  111.5 6.6 %collective-permute-start.9 = (bf16[1,32,512]{2,1,0:T(8,128)(2,1)S(1)}, bf16[1,32,512]{2,1,0:T(8,128)(2,1)S(1)}, u32[]{:S(2)}, u32[]{:S(2)}) collective-permute-start(bf16[1,32,512]{2,1,0:T(8,128)(2,1)S(1)} %collective-permute-done.7), channel_id=1, source_target_pairs={{0,28},{4,0},{8,4},{12,8},{16,12},{20,16},{24,20},{28,24},{1,29},{... | collective-permute-start | bytes 98312 | tf_op jit(solution)/shard_map/ppermute | solution.py:19
  118.1 6.6 %collective-permute-start.12 = (bf16[1,32,512]{2,1,0:T(8,128)(2,1)S(1)}, bf16[1,32,512]{2,1,0:T(8,128)(2,1)S(1)}, u32[]{:S(2)}, u32[]{:S(2)}) collective-permute-start(bf16[1,32,512]{2,1,0:T(8,128)(2,1)S(1)} %collective-permute-done.10), channel_id=1, source_target_pairs={{0,4},{4,8},{8,12},{12,16},{16,20},{20,24},{24,28},{28,0},{1,5},{5... | collective-permute-start | bytes 98312 | tf_op jit(solution)/shard_map/ppermute | solution.py:17
  118.1 6.7 %collective-permute-start.11 = (bf16[1,32,512]{2,1,0:T(8,128)(2,1)S(1)}, bf16[1,32,512]{2,1,0:T(8,128)(2,1)S(1)}, u32[]{:S(2)}, u32[]{:S(2)}) collective-permute-start(bf16[1,32,512]{2,1,0:T(8,128)(2,1)S(1)} %collective-permute-done.9), channel_id=1, source_target_pairs={{0,28},{4,0},{8,4},{12,8},{16,12},{20,16},{24,20},{28,24},{1,29},{... | collective-permute-start | bytes 98312 | tf_op jit(solution)/shard_map/ppermute | solution.py:19
  124.7 6.6 %collective-permute-start.13 = (bf16[1,32,512]{2,1,0:T(8,128)(2,1)S(1)}, bf16[1,32,512]{2,1,0:T(8,128)(2,1)S(1)}, u32[]{:S(2)}, u32[]{:S(2)}) collective-permute-start(bf16[1,32,512]{2,1,0:T(8,128)(2,1)S(1)} %collective-permute-done.12), channel_id=1, source_target_pairs={{0,4},{4,8},{8,12},{12,16},{16,20},{20,24},{24,28},{28,0},{1,5},{5... | collective-permute-start | bytes 98312 | tf_op jit(solution)/shard_map/ppermute | solution.py:17
  140.7 8.6 %copy-start.1 = (bf16[1,2048,512]{2,1,0:T(8,128)(2,1)S(1)}, bf16[1,2048,512]{2,1,0:T(8,128)(2,1)}, u32[]{:S(2)}) copy-start(bf16[1,2048,512]{2,1,0:T(8,128)(2,1)} %get-tuple-element.895) | copy-start | bytes 6291460 | tf_op jit(solution)/shard_map/while
  150.0 8.6 %copy-start.1 = (bf16[1,2048,512]{2,1,0:T(8,128)(2,1)S(1)}, bf16[1,2048,512]{2,1,0:T(8,128)(2,1)}, u32[]{:S(2)}) copy-start(bf16[1,2048,512]{2,1,0:T(8,128)(2,1)} %get-tuple-element.895) | copy-start | bytes 6291460 | tf_op jit(solution)/shard_map/while
  150.0 8.6 %copy-start.4 = (f32[1,512]{1,0:T(1,128)S(1)}, f32[1,512]{1,0:T(1,128)}, u32[]{:S(2)}) copy-start(f32[1,512]{1,0:T(1,128)} %get-tuple-element.889) | copy-start | bytes 6148 | tf_op jit(solution)/shard_map/while
  159.2 8.6 %copy-start.1 = (bf16[1,2048,512]{2,1,0:T(8,128)(2,1)S(1)}, bf16[1,2048,512]{2,1,0:T(8,128)(2,1)}, u32[]{:S(2)}) copy-start(bf16[1,2048,512]{2,1,0:T(8,128)(2,1)} %get-tuple-element.895) | copy-start | bytes 6291460 | tf_op jit(solution)/shard_map/while
  159.2 8.6 %copy-start.4 = (f32[1,512]{1,0:T(1,128)S(1)}, f32[1,512]{1,0:T(1,128)}, u32[]{:S(2)}) copy-start(f32[1,512]{1,0:T(1,128)} %get-tuple-element.889) | copy-start | bytes 6148 | tf_op jit(solution)/shard_map/while
  168.4 8.6 %copy-start.1 = (bf16[1,2048,512]{2,1,0:T(8,128)(2,1)S(1)}, bf16[1,2048,512]{2,1,0:T(8,128)(2,1)}, u32[]{:S(2)}) copy-start(bf16[1,2048,512]{2,1,0:T(8,128)(2,1)} %get-tuple-element.895) | copy-start | bytes 6291460 | tf_op jit(solution)/shard_map/while
  177.7 8.6 %copy-start.1 = (bf16[1,2048,512]{2,1,0:T(8,128)(2,1)S(1)}, bf16[1,2048,512]{2,1,0:T(8,128)(2,1)}, u32[]{:S(2)}) copy-start(bf16[1,2048,512]{2,1,0:T(8,128)(2,1)} %get-tuple-element.895) | copy-start | bytes 6291460 | tf_op jit(solution)/shard_map/while
  186.9 8.6 %copy-start.1 = (bf16[1,2048,512]{2,1,0:T(8,128)(2,1)S(1)}, bf16[1,2048,512]{2,1,0:T(8,128)(2,1)}, u32[]{:S(2)}) copy-start(bf16[1,2048,512]{2,1,0:T(8,128)(2,1)} %get-tuple-element.895) | copy-start | bytes 6291460 | tf_op jit(solution)/shard_map/while
  196.2 8.6 %copy-start.1 = (bf16[1,2048,512]{2,1,0:T(8,128)(2,1)S(1)}, bf16[1,2048,512]{2,1,0:T(8,128)(2,1)}, u32[]{:S(2)}) copy-start(bf16[1,2048,512]{2,1,0:T(8,128)(2,1)} %get-tuple-element.895) | copy-start | bytes 6291460 | tf_op jit(solution)/shard_map/while
  (15 other events, 120.6 us)
